TPU v7x, 128 devices: a whole 4x4x4 slice. The times are simulated.
128 devices in a mesh: seq: 8 (over y, x_hi), hid: 16 (over z, x_lo, core).
Axes of the slice: x: 4 (x_hi: 2, x_lo: 2; x = x_hi * 2 + x_lo), y: 4, z: 4, core: 2. Of those that a mesh axis runs over, the one named last changes fastest.
Arguments:
- tokens: bfloat16 [5120, 5120], P('seq', 'hid'), may hold values from -18 to 18
- clip_id: int32 [5120], P('seq'), may hold values from 0 to 7, never falling along the last dimension, each value on 1 to 3200 neighbouring positions
- clip_step: int32 [8], replicated, may hold values from 0 to 31
- mod_table: float32 [32, 6, 5120], replicated, may hold values from -3 to 3
- w_query: bfloat16 [5120, 4096], P(None, 'hid'), may hold values from -3 to 3
- w_key: bfloat16 [5120, 4096], P(None, 'hid'), may hold values from -3 to 3
- w_value: bfloat16 [5120, 4096], P(None, 'hid'), may hold values from -0.078125 to 0.078125
- q_gain: float32 [4096], P('hid'), may hold values from 0.4 to 6
- k_gain: float32 [4096], P('hid'), may hold values from 0.4 to 6
- w_out: bfloat16 [4096, 5120], P('hid'), may hold values from -0.125 to 0.125
- w_up: bfloat16 [5120, 8192], P(None, 'hid'), may hold values from -0.078125 to 0.078125
- w_down: bfloat16 [8192, 5120], P('hid'), may hold values from -0.09375 to 0.09375
Outputs:
- block_out: bfloat16 [5120, 5120], P('seq', 'hid')
Inputs may be any that keep to these rules, and one draw needn't show every extreme that they name: `clip_id`: clip numbers never fall along the tokens; every clip 0 to 7 holds 1 to 3200 tokens, and one holds exactly 3200.
All inputs are finite; a program needn't handle non-finite values.
Results may differ from a plain program's by a relative error of at most 0.018.
Values may be sent and summed in bfloat16 or wider, within the bound.
A program may use at most 128 MiB of HBM per device.

v0:
```python
import jax
import jax.numpy as jnp
from jax import lax
from jax.sharding import PartitionSpec as P

HEAD_DIM = 128


epsilon = 1e-06
highest = lax.Precision.HIGHEST
masked_low = -1e30


def table_rows(step_hot, mod_table, component, col_start, col_count):
    table = lax.dynamic_slice_in_dim(mod_table[:, component, :], col_start, col_count, 1)
    return jnp.dot(step_hot, table, precision=highest, preferred_element_type=jnp.float32)


def modulated(values, row_mean, spread_sq, scale_rows, shift_rows):
    scaled = (values - row_mean) * lax.rsqrt(spread_sq + epsilon)
    return (scaled * (1.0 + scale_rows) + shift_rows).astype(jnp.bfloat16)


def shared_moments(values, full_width):
    summed, squares = lax.psum((jnp.sum(values, axis=1), jnp.sum(values * values, axis=1)), "hid")
    row_mean = (summed / full_width)[:, None]
    return (row_mean, (squares / full_width)[:, None] - row_mean * row_mean)


def stored(values):
    return lax.optimization_barrier(values.astype(jnp.bfloat16)).astype(jnp.float32)


def shards(
    tokens,
    clip_id,
    clip_step,
    mod_table,
    w_query,
    w_key,
    w_value,
    q_gain,
    k_gain,
    w_out,
    w_up,
    w_down,
):
    tok_rows, feat_part = tokens.shape
    full_width = mod_table.shape[2]
    col_start = lax.axis_index("hid") * feat_part
    head_cols = w_query.shape[1]
    heads_here = head_cols // HEAD_DIM
    all_cols = head_cols * lax.axis_size("hid")
    clip_hot = (
        clip_id[:, None] == jnp.arange(clip_step.shape[0], dtype=jnp.int32)[None, :]
    ).astype(jnp.float32)
    token_step = jnp.dot(
        clip_hot,
        clip_step.astype(jnp.float32),
        precision=highest,
        preferred_element_type=jnp.float32,
    )
    step_hot = (
        token_step[:, None] == jnp.arange(mod_table.shape[0], dtype=jnp.float32)[None, :]
    ).astype(jnp.float32)
    own_rows = tokens.astype(jnp.float32)
    gate_ffn = table_rows(step_hot, mod_table, 5, col_start, feat_part)
    row_mean, spread_sq = shared_moments(own_rows, full_width)
    normed = modulated(
        own_rows,
        row_mean,
        spread_sq,
        table_rows(step_hot, mod_table, 1, col_start, feat_part),
        table_rows(step_hot, mod_table, 0, col_start, feat_part),
    )
    pieces = lax.all_gather(normed, "hid", axis=1, tiled=True)

    def accumulate(weight):
        return jnp.dot(pieces, weight, preferred_element_type=jnp.float32)

    queries = accumulate(w_query)
    key_proj = accumulate(w_key)
    value_proj = accumulate(w_value)
    q_sq, k_sq = lax.psum(
        (jnp.sum(queries * queries, axis=1), jnp.sum(key_proj * key_proj, axis=1)), "hid"
    )
    q_normed = (queries * lax.rsqrt(q_sq / all_cols + epsilon)[:, None] * q_gain).astype(
        jnp.bfloat16
    )
    k_normed = (key_proj * lax.rsqrt(k_sq / all_cols + epsilon)[:, None] * k_gain).astype(
        jnp.bfloat16
    )
    value_rows = value_proj.astype(jnp.bfloat16)
    clip_marks = clip_id.astype(jnp.bfloat16)
    q_heads = q_normed.reshape(tok_rows, heads_here, HEAD_DIM)
    score_scale = HEAD_DIM ** (-0.5)

    def tile_update(running, tile):
        key_tile, value_tile, mark_tile = tile
        old_best, old_sum, old_acc = running
        scores = (
            jnp.einsum("qhd,khd->hqk", q_heads, key_tile, preferred_element_type=jnp.float32)
            * score_scale
        )
        same_clip = (clip_marks[:, None] == mark_tile[None, :])[None]
        masked = jnp.where(same_clip, scores, masked_low)
        row_best = jnp.maximum(old_best, jnp.max(masked, axis=2))
        weights = jnp.where(same_clip, jnp.exp(masked - row_best[:, :, None]), 0.0)
        rescale = jnp.exp(old_best - row_best)
        new_sum = old_sum * rescale + jnp.sum(weights, axis=2)
        mixed = jnp.einsum(
            "hqk,khd->hqd",
            weights.astype(jnp.bfloat16),
            value_tile,
            preferred_element_type=jnp.float32,
        )
        return (row_best, new_sum, old_acc * rescale[:, :, None] + mixed)

    start_state = (
        jnp.full((heads_here, tok_rows), masked_low, jnp.float32),
        jnp.zeros((heads_here, tok_rows), jnp.float32),
        jnp.zeros((heads_here, tok_rows, HEAD_DIM), jnp.float32),
    )
    key_piece = lax.all_gather(k_normed, "seq", axis=0, tiled=True)
    value_piece = lax.all_gather(value_rows, "seq", axis=0, tiled=True)
    mark_piece = lax.all_gather(clip_marks, "seq", axis=0, tiled=True)
    tile_count = key_piece.shape[0] // tok_rows
    tiles = (
        key_piece.reshape(tile_count, tok_rows, heads_here, HEAD_DIM),
        value_piece.reshape(tile_count, tok_rows, heads_here, HEAD_DIM),
        mark_piece.reshape(tile_count, tok_rows),
    )

    def tile_step(inner, tile):
        return (tile_update(inner, tile), None)

    finished, unused = lax.scan(tile_step, start_state, tiles)
    best_all, sum_all, acc_all = finished
    attended = (
        (acc_all / sum_all[:, :, None])
        .astype(jnp.bfloat16)
        .transpose(1, 0, 2)
        .reshape(tok_rows, head_cols)
    )
    out_terms = jnp.dot(attended, w_out, preferred_element_type=jnp.float32)
    attn_own = lax.psum_scatter(
        out_terms.astype(jnp.bfloat16), "hid", scatter_dimension=1, tiled=True
    ).astype(jnp.float32)
    gate_attn = table_rows(step_hot, mod_table, 2, col_start, feat_part)
    residual_own = stored(own_rows + gate_attn * attn_own)
    row_mean, spread_sq = shared_moments(residual_own, full_width)
    normed_ffn = modulated(
        residual_own,
        row_mean,
        spread_sq,
        table_rows(step_hot, mod_table, 4, col_start, feat_part),
        table_rows(step_hot, mod_table, 3, col_start, feat_part),
    )
    up_proj = jnp.dot(
        lax.all_gather(normed_ffn, "hid", axis=1, tiled=True),
        w_up,
        preferred_element_type=jnp.float32,
    )
    hidden = jax.nn.gelu(up_proj, approximate=True).astype(jnp.bfloat16)
    ffn_own = lax.psum_scatter(
        jnp.dot(hidden, w_down, preferred_element_type=jnp.float32).astype(jnp.bfloat16),
        "hid",
        scatter_dimension=1,
        tiled=True,
    ).astype(jnp.float32)
    return (residual_own + gate_ffn * ffn_own).astype(jnp.bfloat16)


def solution(mesh):
    placed = (
        P("seq", "hid"),
        P("seq"),
        P(),
        P(),
        P(None, "hid"),
        P(None, "hid"),
        P(None, "hid"),
        P("hid"),
        P("hid"),
        P("hid", None),
        P(None, "hid"),
        P("hid", None),
    )
    return jax.shard_map(
        shards, mesh=mesh, in_specs=placed, out_specs=P("seq", "hid"), check_vma=False
    )
```

profile of v0, /device:TPU:1, one launch (start us, length us, event | category | flops | bytes accessed | tf_op | source)
XLA Modules:
  0.0 603.4 jit_solution(17240052192492611231)
XLA Ops:
  7.9 4.1 fusion.72
  11.9 29.7 %all-reduce.2 = (f32[640]{0:T(1024)S(1)}, f32[640]{0:T(1024)S(1)}) all-reduce(f32[640]{0:T(1024)S(1)} %get-tuple-element.124, f32[640]{0:T(1024)S(1)} %get-tuple-element.123), channel_id=1, replica_groups=mesh['seq'=8,'hid'=16] {'hid'}, use_global_device_ids=true, to_apply=%region_3.0 | all-reduce | flops 1280 | bytes 10240 | tf_op jit(solution)/shard_map/psum | solution.py:25
  43.7 2.3 fusion.28
  46.1 45.8 %all-gather.6.cloned.1.call-done = bf16[640,5120]{0,1:T(8,128)(2,1)} async-done(((bf16[640,320]{0,1:T(8,128)(2,1)}), bf16[640,5120]{0,1:T(8,128)(2,1)}) %all-gather.6.cloned.1.call-update) | async-done | bytes 6553616 | tf_op jit(solution)/shard_map/all_gather | solution.py:76
  91.9 6.0 multiply_reduce_fusion.1
  98.1 3.1 multiply_reduce_fusion
  101.2 27.2 %all-reduce.1 = (f32[640]{0:T(1024)S(1)}, f32[640]{0:T(1024)S(1)}) all-reduce(f32[640]{0:T(1024)S(1)} %get-tuple-element.163, f32[640]{0:T(1024)S(1)} %get-tuple-element.165), channel_id=1, replica_groups=mesh['seq'=8,'hid'=16] {'hid'}, use_global_device_ids=true, to_apply=%region_5.0 | all-reduce | flops 1280 | bytes 10240 | tf_op jit(solution)/shard_map/psum | solution.py:84
  129.4 6.3 %convolution_convert_fusion.2 = bf16[640,256]{1,0:T(8,128)(2,1)} fusion(bf16[640,5120]{0,1:T(8,128)(2,1)} %all-gather.6.cloned.1.call-done, bf16[5120,256]{1,0:T(8,128)(2,1)} %param.20), kind=kOutput, calls=%fused_computation.56 | convolution fusion | flops 1677885440 | bytes 9502720 | tf_op jit(solution)/shard_map/dot_general | solution.py:79
  135.8 27.8 %all-gather = bf16[8,1,640]{2,1,0:T(2,128)(2,1)S(1)} all-gather(bf16[1,1,640]{2,1,0:T(2,128)(2,1)S(1)} %reshape.75), channel_id=1, replica_groups=mesh['seq'=8,'hid'=16] {'seq'}, dimensions={0}, use_global_device_ids=true | all-gather | bytes 11520 | tf_op jit(solution)/shard_map/all_gather | solution.py:126
  165.1 23.4 %all-gather.8.cloned.1.call-done = bf16[5120,256]{0,1:T(8,128)(2,1)} async-done(((bf16[640,256]{0,1:T(8,128)(2,1)}), bf16[5120,256]{0,1:T(8,128)(2,1)}) %all-gather.8.cloned.1.call-update) | async-done | bytes 2621456 | tf_op jit(solution)/shard_map/all_gather | solution.py:124
  188.5 3.8 copy.35
  192.3 4.8 copy.28
  197.1 49.9 %all-gather.10.cloned.1.call-done = bf16[5120,256]{1,0:T(8,128)(2,1)} async-done(((bf16[640,256]{1,0:T(8,128)(2,1)}), bf16[5120,256]{1,0:T(8,128)(2,1)}) %all-gather.10.cloned.1.call-update) | async-done | bytes 2621456 | tf_op jit(solution)/shard_map/all_gather | solution.py:125
  247.0 4.9 reshape.73
  252.0 84.6 %while.15 = (s32[]{:T(128)}, f32[2,640]{1,0:T(2,128)S(1)}, f32[2,640]{1,0:T(2,128)S(1)}, f32[2,640,128]{2,1,0:T(8,128)}, bf16[640]{0:T(1024)(128)(2,1)S(1)}, /*i...) while((s32[]{:T(128)}, f32[2,640]{1,0:T(2,128)S(1)}, ...), condition=%wide.region_11.12_spmd.clone, body=%wide.region_8.11_spmd.clone.sunk | while | flops 430987520 | bytes 32855764 | solution.py:137
  252.3 3.5 fusion.95
  255.8 2.9 fusion.97
  260.0 1.6 fusion.99
  262.9 3.5 fusion.95
  266.4 2.9 fusion.97
  270.6 1.6 fusion.99
  273.5 3.5 fusion.95
  277.0 2.9 fusion.97
  281.2 1.6 fusion.99
  284.0 3.5 fusion.95
  287.6 2.9 fusion.97
  291.8 1.6 fusion.99
  294.6 3.5 fusion.95
  298.2 2.9 fusion.97
  302.4 1.6 fusion.99
  305.2 3.5 fusion.95
  308.7 2.9 fusion.97
  312.9 1.6 fusion.99
  315.8 3.5 fusion.95
  319.3 2.9 fusion.97
  323.5 1.6 fusion.99
  326.3 3.5 fusion.95
  329.9 2.9 fusion.97
  338.0 5.0 convolution_convert_fusion
  343.1 76.0 %reduce-scatter.3.cloned.1.call-done = bf16[640,320]{0,1:T(8,128)(2,1)} async-done(((bf16[640,5120]{0,1:T(8,128)(2,1)}), bf16[640,320]{0,1:T(8,128)(2,1)}) %reduce-scatter.3.cloned.1.call-update) | async-done | bytes 409616 | tf_op jit(solution)/shard_map/reduce_scatter | solution.py:146
  419.1 1.8 fusion.30
  421.0 29.5 %all-reduce = (f32[640]{0:T(1024)S(1)}, f32[640]{0:T(1024)S(1)}) all-reduce(f32[640]{0:T(1024)S(1)} %get-tuple-element.122, f32[640]{0:T(1024)S(1)} %get-tuple-element.121), channel_id=1, replica_groups=mesh['seq'=8,'hid'=16] {'hid'}, use_global_device_ids=true, to_apply=%region_16.17 | all-reduce | flops 1280 | bytes 10240 | tf_op jit(solution)/shard_map/psum | solution.py:25
  452.2 2.3 fusion.29
  454.8 43.7 %all-gather.12.cloned.1.call-done = bf16[640,5120]{0,1:T(8,128)(2,1)} async-done(((bf16[640,320]{0,1:T(8,128)(2,1)}), bf16[640,5120]{0,1:T(8,128)(2,1)}) %all-gather.12.cloned.1.call-update) | async-done | bytes 6553616 | tf_op jit(solution)/shard_map/all_gather | solution.py:160
  498.5 7.6 %fusion.73 = f32[640,512]{1,0:T(8,128)S(1)} fusion(bf16[640,5120]{0,1:T(8,128)(2,1)} %all-gather.12.cloned.1.call-done, bf16[5120,512]{1,0:T(8,128)(2,1)} %param.24), kind=kOutput, calls=%fused_computation.112 | convolution fusion | flops 3355443200 | bytes 13107200 | tf_op jit(solution)/shard_map/dot_general | solution.py:159
  506.1 9.5 %convolution_convert_fusion.1 = bf16[640,5120]{0,1:T(8,128)(2,1)} fusion(bf16[512,5120]{1,0:T(8,128)(2,1)} %param.25, f32[640,512]{1,0:T(8,128)S(1)} %fusion.73), kind=kOutput, calls=%fused_computation.26 | convolution fusion | flops 3361669120 | bytes 13107200 | tf_op jit(solution)/shard_map/dot_general | solution.py:166
  515.7 78.3 %reduce-scatter.5.cloned.1.call-done = bf16[640,320]{0,1:T(8,128)(2,1)} async-done(((bf16[640,5120]{0,1:T(8,128)(2,1)}), bf16[640,320]{0,1:T(8,128)(2,1)}) %reduce-scatter.5.cloned.1.call-update) | async-done | bytes 409616 | tf_op jit(solution)/shard_map/reduce_scatter | solution.py:165
  594.0 2.6 fusion.31
  (147 shorter events, 30.4 us)
Async XLA Ops:
  6.5 331.4 %copy-start = (bf16[256,5120]{1,0:T(8,128)(2,1)S(1)}, bf16[256,5120]{1,0:T(8,128)(2,1)}, u32[]{:S(2)}) copy-start(bf16[256,5120]{1,0:T(8,128)(2,1)} %param.23) | copy-start | bytes 7864324
  6.5 85.4 %all-gather.6.cloned.1.call-start = ((), (), s32[]{:S(2)}) async-start(), calls=%async_computation.2 | async-start | bytes 6963200 | tf_op jit(solution)/shard_map/all_gather | solution.py:76
  7.8 33.8 %copy-start.7 = (s32[640]{0:T(1024)S(1)}, s32[640]{0:T(1024)}, u32[]{:S(2)}) copy-start(s32[640]{0:T(1024)} %param.15) | copy-start | bytes 7684
  7.8 33.8 %copy-start.11 = (s32[8]{0:T(128)S(1)}, s32[8]{0:T(128)}, u32[]{:S(2)}) copy-start(s32[8]{0:T(128)} %param.16) | copy-start | bytes 100
  7.8 34.2 %copy-start.3 = (bf16[640,320]{0,1:T(8,128)(2,1)S(1)}, bf16[640,320]{0,1:T(8,128)(2,1)}, u32[]{:S(2)}) copy-start(bf16[640,320]{0,1:T(8,128)(2,1)} %param.14) | copy-start | bytes 1228804
  46.0 142.5 %all-gather.8.cloned.1.call-start = ((), (), s32[]{:S(2)}) async-start(), calls=%async_computation.3 | async-start | bytes 2949120 | tf_op jit(solution)/shard_map/all_gather | solution.py:124
  91.9 6.0 copy-start.2
  91.9 6.2 %copy-start.10 = (bf16[5120,256]{1,0:T(8,128)(2,1)S(1)}, bf16[5120,256]{1,0:T(8,128)(2,1)}, u32[]{:S(2)}) copy-start(bf16[5120,256]{1,0:T(8,128)(2,1)} %param.18) | copy-start | bytes 7864324
  98.1 30.3 %copy-start.8 = (f32[256]{0:T(256)S(1)}, f32[256]{0:T(256)}, u32[]{:S(2)}) copy-start(f32[256]{0:T(256)} %param.22) | copy-start | bytes 3076
  129.3 34.3 %copy-start.9 = (f32[256]{0:T(256)S(1)}, f32[256]{0:T(256)}, u32[]{:S(2)}) copy-start(f32[256]{0:T(256)} %param.21) | copy-start | bytes 3076
  129.3 117.7 %all-gather.10.cloned.1.call-start = ((), (), s32[]{:S(2)}) async-start(), calls=%async_computation.4 | async-start | bytes 2949120 | tf_op jit(solution)/shard_map/all_gather | solution.py:125
  135.7 283.4 %reduce-scatter.3.cloned.1.call-start = ((), (), s32[]{:S(2)}) async-start(), calls=%async_computation.5 | async-start | bytes 6963200 | tf_op jit(solution)/shard_map/reduce_scatter | solution.py:146
  255.8 4.2 copy-start.1
  255.8 4.2 copy-start.5
  261.7 0.8 copy-start.6
  266.4 4.2 copy-start.1
  266.4 4.2 copy-start.5
  272.3 0.8 copy-start.6
  277.0 4.2 copy-start.1
  277.0 4.2 copy-start.5
  282.8 0.8 copy-start.6
  287.6 4.2 copy-start.1
  287.6 4.2 copy-start.5
  293.4 0.8 copy-start.6
  298.2 4.2 copy-start.1
  298.2 4.2 copy-start.5
  304.0 0.8 copy-start.6
  308.7 4.2 copy-start.1
  308.7 4.2 copy-start.5
  314.6 0.8 copy-start.6
  319.3 4.2 copy-start.1
  319.3 4.2 copy-start.5
  325.2 0.8 copy-start.6
  329.9 4.2 copy-start.1
  329.9 4.2 copy-start.5
  335.7 0.8 copy-start.6
  343.0 76.1 %copy-start.4 = (bf16[640,320]{0,1:T(8,128)(2,1)S(1)}, bf16[640,320]{0,1:T(8,128)(2,1)}, u32[]{:S(2)}) copy-start(bf16[640,320]{0,1:T(8,128)(2,1)} %param.14) | copy-start | bytes 1228804
  343.0 155.5 %all-gather.12.cloned.1.call-start = ((), (), s32[]{:S(2)}) async-start(), calls=%async_computation.6 | async-start | bytes 6963200 | tf_op jit(solution)/shard_map/all_gather | solution.py:160
  454.6 139.5 %reduce-scatter.5.cloned.1.call-start = ((), (), s32[]{:S(2)}) async-start(), calls=%async_computation.7 | async-start | bytes 6963200 | tf_op jit(solution)/shard_map/reduce_scatter | solution.py:165
Sparse Core Ops, SparseCore 0:
  46.1 45.7 all-gather.5
  129.5 59.0 all-gather.7
  190.8 56.1 all-gather.9
  343.2 75.9 reduce-scatter.2
  454.7 43.7 all-gather.11
  515.8 78.1 reduce-scatter.4
where the time goes:
time: 606 us; the launch traced here: 603 us
  waiting for transfers between devices  317 us (52%)
  blocking collectives  114 us (19%)
  matrix products  91.5 us (15%)
  local copies, waits for them, and re-layouts  36 us (6%)
  other arithmetic  29.8 us (5%)
  between operations  13.7 us (2%)
    reduce_scatter x1, waiting for transfers between devices, shards(): lax.psum_scatter(jnp.dot(hidden, w_down, preferred_element_type=jnp.float...  78.3 us
    reduce_scatter x1, waiting for transfers between devices, shards(): lax.psum_scatter(out_terms.astype(jnp.bfloat16), 'hid', scatter_dimension...  76 us
    psum x2, blocking collectives, shared_moments(): lax.psum((jnp.sum(values, axis=1), jnp.sum(values * values, axis=1)), 'hid')  59.2 us
    all_gather x1, waiting for transfers between devices, shards(): value_piece = lax.all_gather(value_rows, 'seq', axis=0, tiled=True)  49.9 us
    all_gather x1, waiting for transfers between devices, shards(): pieces = lax.all_gather(normed, 'hid', axis=1, tiled=True)  45.8 us
    all_gather x1, waiting for transfers between devices, shards(): lax.all_gather(normed_ffn, 'hid', axis=1, tiled=True)  43.7 us
    dot_general x8, matrix products, tile_update(): jnp.einsum('qhd,khd->hqk', q_heads, key_tile, preferred_element_type=jnp....  28.3 us
    all_gather x1, blocking collectives, shards(): mark_piece = lax.all_gather(clip_marks, 'seq', axis=0, tiled=True)  27.8 us
  transfers between devices with their start and end apart: 6, of which 6 were waited for; matrix products, arithmetic and copies ran while one was open for 3% of the time, Pallas kernels for 0%

commit v1 on v0

--- a/solution.py
+++ b/solution.py
@@ -1,8 +1,298 @@
+import functools
 import jax
 import jax.numpy as jnp
 from jax import lax
+from jax.experimental import pallas as pl
+from jax.experimental.pallas import tpu as pltpu
+
+MESH = pl.DeviceIdType.MESH
+HIGHEST = lax.Precision.HIGHEST
+EPS = 1e-06
+F32 = jnp.float32
+BF16 = jnp.bfloat16
+ANYSPEC = pl.BlockSpec(memory_space=pl.ANY)
+VSPEC = pl.BlockSpec(memory_space=pltpu.VMEM)
+
+OWN, XP, ZM, ZP, ZMX, ZPX, Z2, Z2X = range(8)
+OFFSETS = ((0, 0), (0, 1), (3, 0), (1, 0), (3, 1), (1, 1), (2, 0), (2, 1))
+BACK = (OWN, XP, ZP, ZM, ZPX, ZMX, Z2, Z2X)
+
+
+def hid_place():
+    h = lax.axis_index("hid")
+    return h // 4, lax.rem(h // 2, 2), lax.rem(h, 2)
+
+
+def chip_of(role):
+    z, x, _ = hid_place()
+    dz, dx = OFFSETS[role]
+    return lax.rem(z + dz, 4) * 2 + lax.rem(x + dx, 2)
+
+
+def hid_device(role, flip):
+    core = hid_place()[2]
+    core = 1 - core if flip else core
+    return {"hid": chip_of(role) * 2 + core}
+
+
+def rows_to_columns(rows, width):
+    n = rows.shape[0]
+    pick = (
+        lax.broadcasted_iota(jnp.int32, (n, n * width), 1) // width
+        == lax.broadcasted_iota(jnp.int32, (n, n * width), 0)
+    ).astype(F32)
+    return lax.dot_general(rows, pick, (((0,), (0,)), ((), ())), precision=HIGHEST, preferred_element_type=F32)
+
+
+def lane_sums(values):
+    ones = jnp.ones((8, values.shape[1]), F32)
+    return lax.dot_general(ones, values, (((1,), (1,)), ((), ())), precision=HIGHEST, preferred_element_type=F32)[0:1]
+
+
+def three_way(values):
+    high = values.astype(BF16).astype(F32)
+    rest = values - high
+    middle = rest.astype(BF16).astype(F32)
+    return jnp.concatenate([high, middle, rest - middle], axis=0).astype(BF16)
+
+
+def gather_kernel(kind, widths, x_ref, hot_ref, mod_ref, *refs):
+    nw = len(widths)
+    w_refs, refs = refs[:nw], refs[nw:]
+    if kind == "qkv":
+        qg_ref, kg_ref, q_ref, k_ref, v_ref = refs[:5]
+        refs = refs[5:]
+    else:
+        out_ref = refs[0]
+        refs = refs[1:]
+    (raw, nrm, pair, stat, wbuf, acc, wsem, psem, ssem, rsend, rrecv, dsend, drecv) = refs[:13]
+    refs = refs[13:]
+    half, full = raw.shape[1], raw.shape[2]
+    part = full // 2
+    quarter = half // 2
+    core = hid_place()[2]
+    total_w = sum(widths)
+
+    w_copies = {}
+    for role in (OWN, ZM, ZP, XP, Z2, ZMX, ZPX, Z2X):
+        at = 0
+        for i in range(nw):
+            cp = pltpu.make_async_copy(
+                w_refs[i].at[pl.ds(chip_of(role) * full, full)],
+                wbuf.at[role, :, pl.ds(at, widths[i])],
+                wsem.at[role, i],
+            )
+            cp.start()
+            w_copies[role, i] = cp
+            at += widths[i]
+
+    barrier = pltpu.get_barrier_semaphore()
+    n_peers = 8 if kind != "qkv" else 15
+    pl.semaphore_signal(barrier, inc=1, device_id=hid_device(OWN, True), device_id_type=MESH)
+    for role in range(1, 8):
+        pl.semaphore_signal(barrier, inc=1, device_id=hid_device(role, False), device_id_type=MESH)
+        if kind == "qkv":
+            pl.semaphore_signal(barrier, inc=1, device_id=hid_device(role, True), device_id_type=MESH)
+    pl.semaphore_wait(barrier, n_peers)
+
+    swap = pltpu.make_async_remote_copy(
+        x_ref.at[pl.ds((1 - core) * half, half)], pair, psem.at[0], psem.at[1],
+        device_id=hid_device(OWN, True), device_id_type=MESH,
+    )
+    swap.start()
+    sends = []
+
+    def place(shift):
+        rows = lax.broadcasted_iota(jnp.int32, (part, full), 0)
+        cols = lax.broadcasted_iota(jnp.int32, (part, full), 1)
+        return (cols == rows + shift).astype(F32).astype(BF16)
+
+    mine = jnp.dot(x_ref[pl.ds(core * half, half)], place(core * part), preferred_element_type=F32)
+    swap.wait_recv()
+    block = mine + jnp.dot(pair[...], place((1 - core) * part), preferred_element_type=F32)
+    raw[OWN] = block.astype(BF16)
+
+    def send_raw(slot, lo, count, to_role, to_slot, sem):
+        cp = pltpu.make_async_remote_copy(
+            raw.at[slot, pl.ds(lo, count)], raw.at[to_slot, pl.ds(lo, count)],
+            rsend.at[sem], rrecv.at[sem],
+            device_id=hid_device(to_role, False), device_id_type=MESH,
+        )
+        cp.start()
+        sends.append(cp)
+        return cp
+
+    to_zp = send_raw(OWN, 0, half, ZP, ZM, ZM)
+    to_zm = send_raw(OWN, 0, half, ZM, ZP, ZP)
+    to_x = send_raw(OWN, 0, half, XP, XP, XP)
+
+    stat[OWN, 0:1] = lane_sums(block)
+    stat[OWN, 1:2] = lane_sums(block * block)
+    stat_copies = []
+    for role in range(1, 8):
+        cp = pltpu.make_async_remote_copy(
+            stat.at[OWN], stat.at[BACK[role]], ssem.at[0, role], ssem.at[1, BACK[role]],
+            device_id=hid_device(role, False), device_id_type=MESH,
+        )
+        cp.start()
+        stat_copies.append(cp)
+    for cp in stat_copies:
+        cp.wait()
+    totals = stat[0]
+    for role in range(1, 8):
+        totals = totals + stat[role]
+    width_all = full * 8
+    moments = rows_to_columns(totals * (1.0 / width_all), 128)
+    row_mean = moments[:, 0:1]
+    inv = lax.rsqrt(moments[:, 128:129] - row_mean * row_mean + EPS)
+    hot = hot_ref[pl.ds(core * half, half)]
+    d_copies = {}
+
+    def normalize(role):
+        col = pl.multiple_of(chip_of(role) * full, 128)
+        scale = jnp.dot(hot, three_way(mod_ref[0, :, pl.ds(col, full)]), preferred_element_type=F32)
+        shift = jnp.dot(hot, three_way(mod_ref[1, :, pl.ds(col, full)]), preferred_element_type=F32)
+        values = (raw[role].astype(F32) - row_mean) * inv
+        nrm[core, role] = (values * (1.0 + scale) + shift).astype(BF16)
+        cp = pltpu.make_async_remote_copy(
+            nrm.at[core, role], nrm.at[core, role], dsend.at[role], drecv.at[role],
+            device_id=hid_device(OWN, True), device_id_type=MESH,
+        )
+        cp.start()
+        d_copies[role] = cp
+
+    first = [True, True]
+
+    def multiply(role, which):
+        side = core if which == 0 else 1 - core
+        if which == 0:
+            for i in range(nw):
+                w_copies[role, i].wait()
+        else:
+            d_copies[role].wait_recv()
+        term = jnp.dot(nrm[side, role], wbuf[role], preferred_element_type=F32)
+        if first[which]:
+            acc[side] = term
+        else:
+            acc[side] += term
+        first[which] = False
+
+    normalize(OWN)
+    multiply(OWN, 0)
+    to_zp.wait_recv()
+    send_raw(ZM, 0, quarter, ZP, Z2, Z2)
+    to_zm.wait_recv()
+    send_raw(ZP, quarter, quarter, ZM, Z2, 8)
+    to_x.wait_recv()
+    send_raw(XP, 0, half, ZP, ZMX, ZMX)
+    send_raw(XP, 0, half, ZM, ZPX, ZPX)
+    multiply(OWN, 1)
+    normalize(ZM)
+    multiply(ZM, 0)
+    normalize(ZP)
+    multiply(ZP, 0)
+    multiply(ZM, 1)
+    normalize(XP)
+    multiply(XP, 0)
+    multiply(ZP, 1)
+    sends[3].wait_recv()
+    sends[4].wait_recv()
+    send_raw(Z2, 0, half, XP, Z2X, Z2X)
+    multiply(XP, 1)
+    normalize(Z2)
+    multiply(Z2, 0)
+    multiply(Z2, 1)
+    sends[5].wait_recv()
+    normalize(ZMX)
+    multiply(ZMX, 0)
+    sends[6].wait_recv()
+    normalize(ZPX)
+    multiply(ZPX, 0)
+    multiply(ZMX, 1)
+    sends[7].wait_recv()
+    normalize(Z2X)
+    multiply(Z2X, 0)
+    multiply(ZPX, 1)
+    multiply(Z2X, 1)
+
+    swap.wait_send()
+    for cp in sends:
+        cp.wait_send()
+    for role in range(8):
+        d_copies[role].wait_send()
+
+    if kind != "qkv":
+        for side in range(2):
+            out_ref[pl.ds(side * half, half)] = jax.nn.gelu(acc[side], approximate=True).astype(BF16)
+        return
+
+    qstat, qsend, qrecv = refs
+    wq = widths[0]
+    for side in range(2):
+        q = acc[side, :, 0:wq]
+        k = acc[side, :, wq:2 * wq]
+        qstat[0, 2 * side:2 * side + 1] = lane_sums(q * q)
+        qstat[0, 2 * side + 1:2 * side + 2] = lane_sums(k * k)
+        v_ref[pl.ds(side * half, half)] = acc[side, :, 2 * wq:3 * wq].astype(BF16)
+    copies = []
+    for flip in (False, True):
+        for role in range(8):
+            if role == OWN and not flip:
+                continue
+            cp = pltpu.make_async_remote_copy(
+                qstat.at[0], qstat.at[BACK[role] + 8 * flip], qsend.at[role + 8 * flip], qrecv.at[BACK[role] + 8 * flip],
+                device_id=hid_device(role, flip), device_id_type=MESH,
+            )
+            cp.start()
+            copies.append(cp)
+    for cp in copies:
+        cp.wait()
+    sums = qstat[0]
+    for i in range(1, 16):
+        sums = sums + qstat[i]
+    scales = lax.rsqrt(rows_to_columns(sums * (1.0 / (16 * wq)), 128) + EPS)
+    for side in range(2):
+        at = side * 256
+        q_ref[pl.ds(side * half, half)] = (acc[side, :, 0:wq] * scales[:, at:at + 1] * qg_ref[...]).astype(BF16)
+        k_ref[pl.ds(side * half, half)] = (acc[side, :, wq:2 * wq] * scales[:, at + 128:at + 129] * kg_ref[...]).astype(BF16)
+
+
+def gather_project(kind, x, hot, mod, weights, gains, cid):
+    rows, part = x.shape
+    half, full = rows // 2, 2 * part
+    widths = tuple(w.shape[1] for w in weights)
+    total = sum(widths)
+    if kind == "qkv":
+        outs = [jax.ShapeDtypeStruct((rows, w), BF16) for w in widths]
+        extra = [pltpu.VMEM((16, 4, half), F32), pltpu.SemaphoreType.DMA((16,)), pltpu.SemaphoreType.DMA((16,))]
+    else:
+        outs = [jax.ShapeDtypeStruct((rows, total), BF16)]
+        extra = []
+    res = pl.pallas_call(
+        functools.partial(gather_kernel, kind, widths),
+        out_shape=outs,
+        in_specs=[VSPEC, VSPEC, VSPEC] + [ANYSPEC] * len(weights) + [VSPEC] * len(gains),
+        out_specs=[VSPEC] * len(outs),
+        scratch_shapes=[
+            pltpu.VMEM((8, half, full), BF16),
+            pltpu.VMEM((2, 8, half, full), BF16),
+            pltpu.VMEM((half, part), BF16),
+            pltpu.VMEM((8, 2, half), F32),
+            pltpu.VMEM((8, full, total), BF16),
+            pltpu.VMEM((2, half, total), F32),
+            pltpu.SemaphoreType.DMA((8, len(weights))),
+            pltpu.SemaphoreType.DMA((2,)),
+            pltpu.SemaphoreType.DMA((2, 8)),
+            pltpu.SemaphoreType.DMA((9,)),
+            pltpu.SemaphoreType.DMA((9,)),
+            pltpu.SemaphoreType.DMA((8,)),
+            pltpu.SemaphoreType.DMA((8,)),
+        ] + extra,
+        compiler_params=pltpu.CompilerParams(collective_id=cid, has_side_effects=True, vmem_limit_bytes=56 << 20),
+        name="gather_" + kind,
+    )(x, hot, mod, *weights, *gains)
+    return res
 from jax.sharding import PartitionSpec as P
-
 HEAD_DIM = 128
 
 
@@ -65,32 +355,12 @@
     ).astype(jnp.float32)
     own_rows = tokens.astype(jnp.float32)
     gate_ffn = table_rows(step_hot, mod_table, 5, col_start, feat_part)
-    row_mean, spread_sq = shared_moments(own_rows, full_width)
-    normed = modulated(
-        own_rows,
-        row_mean,
-        spread_sq,
-        table_rows(step_hot, mod_table, 1, col_start, feat_part),
-        table_rows(step_hot, mod_table, 0, col_start, feat_part),
-    )
-    pieces = lax.all_gather(normed, "hid", axis=1, tiled=True)
-
-    def accumulate(weight):
-        return jnp.dot(pieces, weight, preferred_element_type=jnp.float32)
-
-    queries = accumulate(w_query)
-    key_proj = accumulate(w_key)
-    value_proj = accumulate(w_value)
-    q_sq, k_sq = lax.psum(
-        (jnp.sum(queries * queries, axis=1), jnp.sum(key_proj * key_proj, axis=1)), "hid"
-    )
-    q_normed = (queries * lax.rsqrt(q_sq / all_cols + epsilon)[:, None] * q_gain).astype(
-        jnp.bfloat16
-    )
-    k_normed = (key_proj * lax.rsqrt(k_sq / all_cols + epsilon)[:, None] * k_gain).astype(
-        jnp.bfloat16
-    )
-    value_rows = value_proj.astype(jnp.bfloat16)
+    mods = mod_table[clip_step].transpose(1, 0, 2)
+    hot24 = (clip_id[:, None] == jnp.arange(24, dtype=jnp.int32)[None, :] % 8).astype(jnp.bfloat16)
+    q_normed, k_normed, value_rows = gather_project(
+        "qkv", tokens, hot24, jnp.stack([mods[1], mods[0]]), (w_query, w_key, w_value),
+        (q_gain[None, :], k_gain[None, :]), 1,
+    )
     clip_marks = clip_id.astype(jnp.bfloat16)
     q_heads = q_normed.reshape(tok_rows, heads_here, HEAD_DIM)
     score_scale = HEAD_DIM ** (-0.5)

time: 606 us -> 552 us (0.911)
  blocking collectives: 114 us -> 57.7 us
  Pallas kernels: 0 us -> 52 us
  waiting for transfers between devices: 317 us -> 277 us
  matrix products: 91.5 us -> 85.3 us
    pallas_call x0 -> x1, Pallas kernels: none -> 52 us  [gather_project(): pl.pallas_call(functools.partial(gather_kernel, kind, widths), out_shape=...]
    all_gather x1 -> x0, waiting for transfers between devices: 45.8 us -> none  [shards(): pieces = lax.all_gather(normed, 'hid', axis=1, tiled=True)]
    psum x2 -> x1, blocking collectives: 59.2 us -> 29.8 us  [shared_moments(): lax.psum((jnp.sum(values, axis=1), jnp.sum(values * values, axis=1)), 'hid')]
    psum x1 -> x0, blocking collectives: 27.2 us -> none  [shards(): lax.psum((jnp.sum(queries * queries, axis=1), jnp.sum(key_proj * key_proj...]
    dot_general x3 -> x0, matrix products: 15.4 us -> none  [accumulate(): return jnp.dot(pieces, weight, preferred_element_type=jnp.float32)]
    dot_general x8, matrix products: 13 us -> 26.4 us  [tile_update(): jnp.einsum('hqk,khd->hqd', weights.astype(jnp.bfloat16), value_tile, pref...]
    while x56 -> x24, local copies, waits for them, and re-layouts: 6.77 us -> 0.04 us
    dot_general x6 -> x4, matrix products: 12.2 us -> 8.29 us  [table_rows(): jnp.dot(step_hot, table, precision=highest, preferred_element_type=jnp.fl...]
  transfers between devices with their start and end apart: 6 -> 5, of which waited for: 6 -> 5; matrix products, arithmetic and copies ran while one was open for 3% -> 2% of each run, Pallas kernels for 0% -> 0%
where the time goes in v1:
time: 552 us; the launch traced here: 549 us
  waiting for transfers between devices  277 us (50%)
  matrix products  85.3 us (15%)
  blocking collectives  57.7 us (10%)
  Pallas kernels  52 us (9%)
  local copies, waits for them, and re-layouts  34.8 us (6%)
  other arithmetic  28.8 us (5%)
  between operations  13.3 us (2%)
    reduce_scatter x1, waiting for transfers between devices, shards(): lax.psum_scatter(jnp.dot(hidden, w_down, preferred_element_type=jnp.float...  78.3 us
    reduce_scatter x1, waiting for transfers between devices, shards(): lax.psum_scatter(out_terms.astype(jnp.bfloat16), 'hid', scatter_dimension...  71.8 us
    all_gather x1, waiting for transfers between devices, shards(): value_piece = lax.all_gather(value_rows, 'seq', axis=0, tiled=True)  53.6 us
    pallas_call x1, Pallas kernels, gather_project(): pl.pallas_call(functools.partial(gather_kernel, kind, widths), out_shape=...  52 us
    all_gather x1, waiting for transfers between devices, shards(): lax.all_gather(normed_ffn, 'hid', axis=1, tiled=True)  43.8 us
    psum x1, blocking collectives, shared_moments(): lax.psum((jnp.sum(values, axis=1), jnp.sum(values * values, axis=1)), 'hid')  29.8 us
    all_gather x1, waiting for transfers between devices, shards(): key_piece = lax.all_gather(k_normed, 'seq', axis=0, tiled=True)  28.3 us
    dot_general x8, matrix products, tile_update(): jnp.einsum('qhd,khd->hqk', q_heads, key_tile, preferred_element_type=jnp....  28 us
  transfers between devices with their start and end apart: 5, of which 5 were waited for; matrix products, arithmetic and copies ran while one was open for 2% of the time, Pallas kernels for 0%

profile of v1, /device:TPU:1, one launch (start us, length us, event | category | flops | bytes accessed | tf_op | source)
XLA Modules:
  0.0 549.0 jit_solution(12149936501691911409)
XLA Ops:
  7.4 3.5 gather_fusion
  14.4 52.0 %gather_qkv.1 = (bf16[640,256]{1,0:T(8,128)(2,1)}, bf16[640,256]{1,0:T(8,128)(2,1)}, bf16[640,256]{1,0:T(8,128)(2,1)}) custom-call(bf16[640,320]{1,0:T(8,128)(2,1)} %copy.38.x_ref, bf16[640,24]{1,0:T(8,128)(2,1)} %compare_convert_fusion.hot_ref, f32[2,8,5120]{2,1,0:T(8,128)} %pad_maximum_fusion.mod_ref, bf16[5120,256]{1,0:T(8,128)(2,1)} %refs_0_.1, ...), custom_call_target="tpu_custom_call" | custom-call | tf_op jit(solution)/shard_map/gather_qkv/pallas_call | solution.py:271
  67.4 27.9 %all-gather = bf16[8,1,640]{2,1,0:T(2,128)(2,1)S(1)} all-gather(bf16[1,1,640]{2,1,0:T(2,128)(2,1)S(1)} %reshape.87), channel_id=1, replica_groups=mesh['seq'=8,'hid'=16] {'seq'}, dimensions={0}, use_global_device_ids=true | all-gather | bytes 11520 | tf_op jit(solution)/shard_map/all_gather | solution.py:396
  95.3 1.8 copy_bitcast_fusion.4
  97.0 28.3 %all-gather.5.cloned.1.call-done = bf16[5120,256]{1,0:T(8,128)(2,1)} async-done(((bf16[640,256]{1,0:T(8,128)(2,1)}), bf16[5120,256]{1,0:T(8,128)(2,1)}) %all-gather.5.cloned.1.call-update) | async-done | bytes 2621456 | tf_op jit(solution)/shard_map/all_gather | solution.py:394
  125.4 4.9 reshape.74
  130.3 53.6 %all-gather.7.cloned.1.call-done = bf16[5120,256]{1,0:T(8,128)(2,1)} async-done(((bf16[640,256]{1,0:T(8,128)(2,1)}), bf16[5120,256]{1,0:T(8,128)(2,1)}) %all-gather.7.cloned.1.call-update) | async-done | bytes 2621456 | tf_op jit(solution)/shard_map/all_gather | solution.py:395
  183.9 4.9 reshape.76
  188.8 93.4 %while.15 = (s32[]{:T(128)}, f32[2,640]{1,0:T(2,128)S(1)}, f32[2,640]{1,0:T(2,128)S(1)}, f32[2,640,128]{2,1,0:T(8,128)}, bf16[640]{0:T(1024)(128)(2,1)S(1)}, /*i...) while((s32[]{:T(128)}, f32[2,640]{1,0:T(2,128)S(1)}, ...), condition=%wide.region_3.4_spmd.clone, body=%wide.region_0.3_spmd.clone.sunk | while | flops 430987520 | bytes 28267676 | solution.py:407
  189.2 1.5 constant_dynamic-slice_fusion.3
  190.7 3.5 fusion.77
  194.2 2.9 fusion.79
  197.2 2.4 fusion.81
  199.9 1.5 constant_dynamic-slice_fusion.3
  201.4 3.5 fusion.77
  205.0 2.9 fusion.79
  207.9 3.4 fusion.81
  211.7 1.5 constant_dynamic-slice_fusion.3
  213.3 3.5 fusion.77
  216.8 2.9 fusion.79
  219.8 3.4 fusion.81
  225.1 3.5 fusion.77
  228.6 2.9 fusion.79
  231.6 3.4 fusion.81
  236.9 3.5 fusion.77
  240.4 2.9 fusion.79
  243.4 3.4 fusion.81
  248.7 3.5 fusion.77
  252.2 2.9 fusion.79
  255.2 3.4 fusion.81
  260.5 3.5 fusion.77
  264.0 2.9 fusion.79
  267.0 3.4 fusion.81
  272.3 3.5 fusion.77
  275.9 2.9 fusion.79
  278.8 3.4 fusion.81
  283.7 5.0 convolution_convert_fusion
  289.7 3.3 fusion.58
  293.0 71.8 %reduce-scatter.3.cloned.1.call-done = bf16[640,320]{0,1:T(8,128)(2,1)} async-done(((bf16[640,5120]{0,1:T(8,128)(2,1)}), bf16[640,320]{0,1:T(8,128)(2,1)}) %reduce-scatter.3.cloned.1.call-update) | async-done | bytes 409616 | tf_op jit(solution)/shard_map/reduce_scatter | solution.py:416
  364.8 1.8 fusion.25
  366.7 29.8 %all-reduce = (f32[640]{0:T(1024)S(1)}, f32[640]{0:T(1024)S(1)}) all-reduce(f32[640]{0:T(1024)S(1)} %get-tuple-element.137, f32[640]{0:T(1024)S(1)} %get-tuple-element.136), channel_id=1, replica_groups=mesh['seq'=8,'hid'=16] {'hid'}, use_global_device_ids=true, to_apply=%region_8.9 | all-reduce | flops 1280 | bytes 10240 | tf_op jit(solution)/shard_map/psum | solution.py:315
  396.6 1.6 fusion.23
  398.2 2.3 fusion.26
  400.6 43.8 %all-gather.9.cloned.1.call-done = bf16[640,5120]{0,1:T(8,128)(2,1)} async-done(((bf16[640,320]{0,1:T(8,128)(2,1)}), bf16[640,5120]{0,1:T(8,128)(2,1)}) %all-gather.9.cloned.1.call-update) | async-done | bytes 6553616 | tf_op jit(solution)/shard_map/all_gather | solution.py:430
  444.4 7.6 %fusion.60 = f32[640,512]{1,0:T(8,128)S(1)} fusion(bf16[640,5120]{0,1:T(8,128)(2,1)} %all-gather.9.cloned.1.call-done, bf16[5120,512]{1,0:T(8,128)(2,1)} %param.24), kind=kOutput, calls=%fused_computation.93 | convolution fusion | flops 3355443200 | bytes 13107200 | tf_op jit(solution)/shard_map/dot_general | solution.py:429
  452.0 9.6 %convolution_convert_fusion.1 = bf16[640,5120]{0,1:T(8,128)(2,1)} fusion(bf16[512,5120]{1,0:T(8,128)(2,1)} %param.25, f32[640,512]{1,0:T(8,128)S(1)} %fusion.60), kind=kOutput, calls=%fused_computation.26 | convolution fusion | flops 3361669120 | bytes 13107200 | tf_op jit(solution)/shard_map/dot_general | solution.py:436
  461.6 78.3 %reduce-scatter.5.cloned.1.call-done = bf16[640,320]{0,1:T(8,128)(2,1)} async-done(((bf16[640,5120]{0,1:T(8,128)(2,1)}), bf16[640,320]{0,1:T(8,128)(2,1)}) %reduce-scatter.5.cloned.1.call-update) | async-done | bytes 409616 | tf_op jit(solution)/shard_map/reduce_scatter | solution.py:435
  539.9 2.6 fusion.27
  (99 shorter events, 18.4 us)
Async XLA Ops:
  6.5 277.1 %copy-start = (bf16[256,5120]{1,0:T(8,128)(2,1)S(1)}, bf16[256,5120]{1,0:T(8,128)(2,1)}, u32[]{:S(2)}) copy-start(bf16[256,5120]{1,0:T(8,128)(2,1)} %param.23) | copy-start | bytes 7864324
  6.5 118.8 %all-gather.5.cloned.1.call-start = ((), (), s32[]{:S(2)}) async-start(), calls=%async_computation.2 | async-start | bytes 2949120 | tf_op jit(solution)/shard_map/all_gather | solution.py:394
  7.4 4.5 copy-start.2
  7.4 6.3 %copy-start.4 = (s32[640]{0:T(1024)S(1)}, s32[640]{0:T(1024)}, u32[]{:S(2)}) copy-start(s32[640]{0:T(1024)} %param.15) | copy-start | bytes 7684
  66.5 117.4 %all-gather.7.cloned.1.call-start = ((), (), s32[]{:S(2)}) async-start(), calls=%async_computation.3 | async-start | bytes 2949120 | tf_op jit(solution)/shard_map/all_gather | solution.py:395
  67.3 297.5 %reduce-scatter.3.cloned.1.call-start = ((), (), s32[]{:S(2)}) async-start(), calls=%async_computation.4 | async-start | bytes 6963200 | tf_op jit(solution)/shard_map/reduce_scatter | solution.py:416
  194.2 3.0 copy-start.1
  205.0 3.0 copy-start.1
  216.8 3.0 copy-start.1
  228.6 3.0 copy-start.1
  240.4 3.0 copy-start.1
  252.2 3.0 copy-start.1
  264.0 3.0 copy-start.1
  275.8 3.0 copy-start.1
  288.7 0.7 copy-start.5
  288.7 76.1 %copy-start.3 = (bf16[640,320]{0,1:T(8,128)(2,1)S(1)}, bf16[640,320]{0,1:T(8,128)(2,1)}, u32[]{:S(2)}) copy-start(bf16[640,320]{0,1:T(8,128)(2,1)} %param.14) | copy-start | bytes 1228804
  288.7 155.7 %all-gather.9.cloned.1.call-start = ((), (), s32[]{:S(2)}) async-start(), calls=%async_computation.5 | async-start | bytes 6963200 | tf_op jit(solution)/shard_map/all_gather | solution.py:430
  400.5 139.4 %reduce-scatter.5.cloned.1.call-start = ((), (), s32[]{:S(2)}) async-start(), calls=%async_computation.6 | async-start | bytes 6963200 | tf_op jit(solution)/shard_map/reduce_scatter | solution.py:435
Sparse Core Ops, SparseCore 0:
  66.6 58.6 all-gather.4
  127.7 56.2 all-gather.6
  288.8 75.9 reduce-scatter.2
  400.7 43.7 all-gather.8
  461.7 78.1 reduce-scatter.4
